TPU v7x, 32 devices: a whole 2x2x4 slice. The times are simulated.
32 devices in a mesh: grp: 4 (over x, core), ep: 8 (over z, y).
Axes of the slice: x: 2, y: 2, z: 4, core: 2. Of those that a mesh axis runs over, the one named last changes fastest.
Arguments:
- features: bfloat16 [8192, 1152], P(('grp', 'ep')), may hold values from -6 to 6
- token_position: int32 [8192], P(('grp', 'ep')), may hold values from 0 to 2047, as said below
- expert_ids: int32 [8192, 2], P(('grp', 'ep')), may hold values from 0 to 7, all different within a row; in each aligned block of 256 rows (0 to 255, 256 to 511, ...) at most 128 rows name the same one
- proj_in: bfloat16 [1152, 2560], P('ep'), may hold values from -0.1875 to 0.1875
- bias_in: float32 [2560], replicated, may hold values from -3 to 3
- proj_out: bfloat16 [2560, 2560], P('ep'), may hold values from -0.125 to 0.125
- bias_out: float32 [2560], replicated, may hold values from -3 to 3
- norm_gain: float32 [2560], replicated, may hold values from 0.1 to 1.9
- router: bfloat16 [2560, 8], replicated, may hold values from -0.125 to 0.125
- w_gate: bfloat16 [8, 2560, 512], P('ep'), may hold values from -0.125 to 0.125
- w_up: bfloat16 [8, 2560, 512], P('ep'), may hold values from -0.125 to 0.125
- w_down: bfloat16 [8, 512, 2560], P('ep'), may hold values from -0.25 to 0.25
Outputs:
- mixed: bfloat16 [8192, 2560], P(('grp', 'ep'))
Inputs may be any that keep to these rules, and one draw needn't show every extreme that they name: `token_position`: within each group of 8 devices along ep, the group's values form a permutation of 0 to 2047; position q belongs to the device of ep index q // 256. The rows of each device hold exactly 32 positions of every device of its group. `expert_ids`: each row names 2 different experts; no expert is named by more than 128 of the rows of one device.
All inputs are finite; a program needn't handle non-finite values.
Results may differ from a plain program's by a relative error of at most 0.0071.
Values may be sent and summed in bfloat16 or wider, within the bound.
A program may use at most 192 MiB of HBM per device.

v0:
```python
import jax
import jax.numpy as jnp
from jax import lax
from jax.sharding import PartitionSpec as P

EPSILON = 1e-06
F32 = jnp.float32
BF16 = jnp.bfloat16


def select_rows(mask, rows):
    return jnp.dot(mask.astype(BF16), rows, preferred_element_type=F32).astype(BF16)


def gather_columns(weight):
    members = lax.axis_size("grp")
    width = weight.shape[1] // members
    part = lax.dynamic_slice_in_dim(weight, lax.axis_index("grp") * width, width, 1)
    full = lax.all_gather(part, ("grp", "ep"), axis=0, tiled=True)
    return full.reshape(members, -1, width)


def shards(
    features,
    token_position,
    expert_ids,
    proj_in,
    bias_in,
    proj_out,
    bias_out,
    norm_gain,
    router,
    w_gate,
    w_up,
    w_down,
):
    members = lax.axis_size("ep")
    row_count, vis = features.shape
    width = proj_in.shape[1]
    first_full = gather_columns(proj_in)
    second_full = gather_columns(proj_out)
    index = jnp.arange(row_count, dtype=jnp.int32)
    rank = jnp.sum((token_position[None, :] < token_position[:, None]).astype(jnp.int32), axis=1)
    local = token_position % row_count
    lane = jnp.arange(128, dtype=jnp.int32)[None, :]
    high, low = ((local // 16)[:, None], (local % 16)[:, None])
    tail = jnp.where(lane == 0, high, jnp.where(lane == 1, low, 0)).astype(BF16)
    order = rank[None, :] == index[:, None]
    sent = select_rows(order, jnp.concatenate([features, tail], axis=1))
    arrived = lax.all_to_all(sent, "ep", split_axis=0, concat_axis=0, tiled=True)
    landing = (arrived[:, vis].astype(F32) * 16 + arrived[:, vis + 1].astype(F32)).astype(jnp.int32)
    patches = select_rows(landing[None, :] == index[:, None], arrived[:, :vis])
    pre_act = jnp.einsum("rk,gkn->rgn", patches, first_full, preferred_element_type=F32)
    pre_act = pre_act.reshape(row_count, width)
    hidden = jax.nn.gelu(pre_act + bias_in, approximate=False).astype(BF16)
    result = jnp.einsum("rk,gkn->rgn", hidden, second_full, preferred_element_type=F32)
    tokens = (result.reshape(row_count, width) + bias_out).astype(BF16)
    wide = tokens.astype(F32)
    scale = lax.rsqrt(jnp.mean(wide * wide, axis=-1, keepdims=True) + EPSILON)
    normed = (wide * scale * norm_gain).astype(BF16)
    experts = router.shape[1]
    top_count = expert_ids.shape[1]
    capacity = 2 * row_count * top_count // experts
    local_experts = w_gate.shape[0]
    logits = jnp.dot(normed, router, preferred_element_type=F32)
    numbers = jnp.arange(experts, dtype=jnp.int32)
    chosen_mask = expert_ids[:, :, None] == numbers[None, None, :]
    chosen = jnp.sum(jnp.where(chosen_mask, logits[:, None, :], 0.0), axis=2)
    first_gate = jax.nn.sigmoid(chosen[:, 0] - chosen[:, 1])
    gates = (first_gate, 1.0 - first_gate)
    named = jnp.any(chosen_mask, axis=1)
    earlier = (index[None, :] < index[:, None]).astype(BF16)
    before = jnp.dot(earlier, named.astype(BF16), preferred_element_type=F32).astype(jnp.int32)
    place = jnp.where(named, before, -1)
    slots = jnp.arange(capacity, dtype=jnp.int32)
    filled = place.T[:, None, :] == slots[None, :, None]
    blocks = select_rows(filled.reshape(experts * capacity, row_count), normed)
    blocks = blocks.reshape(members, local_experts, capacity, width)
    received = lax.all_to_all(blocks, "ep", split_axis=0, concat_axis=0, tiled=True)
    gate_part = jnp.einsum("pecd,edf->pecf", received, w_gate, preferred_element_type=F32)
    up_part = jnp.einsum("pecd,edf->pecf", received, w_up, preferred_element_type=F32)
    activated = (jax.nn.silu(gate_part) * up_part).astype(BF16)
    outputs = jnp.einsum("pecf,efd->pecd", activated, w_down, preferred_element_type=F32).astype(
        BF16
    )
    returned = lax.all_to_all(outputs, "ep", split_axis=0, concat_axis=0, tiled=True)
    returned = returned.reshape(experts * capacity, width)
    total = 0.0
    for choice in range(top_count):
        slot = jnp.where(chosen_mask[:, choice], before, -1)
        picked = (slot[:, :, None] == slots[None, None, :]).reshape(row_count, experts * capacity)
        row = jnp.dot(picked.astype(BF16), returned, preferred_element_type=F32)
        total = total + gates[choice][:, None] * row
    return (wide + total).astype(BF16)


def solution(mesh):
    placed = (
        P(("grp", "ep"), None),
        P(("grp", "ep")),
        P(("grp", "ep"), None),
        P("ep", None),
        P(),
        P("ep", None),
        P(),
        P(),
        P(),
        P("ep", None, None),
        P("ep", None, None),
        P("ep", None, None),
    )
    return jax.shard_map(
        shards, mesh=mesh, in_specs=placed, out_specs=P(("grp", "ep"), None), check_vma=False
    )
```

profile of v0, /device:TPU:0, one launch (start us, length us, event | category | flops | bytes accessed | tf_op | source)
XLA Modules:
  0.0 494.2 jit_solution(15530253404360054965)
XLA Ops:
  6.5 0.0 copy-start
  6.5 0.0 all-gather.3.cloned.1.call-start
  6.5 1.8 constant_dynamic-slice_fusion.1
  8.3 0.0 all-gather.3.cloned.1.call-update
  8.4 0.0 all-gather.5.cloned.1.call-start
  8.4 1.8 constant_dynamic-slice_fusion
  10.2 0.0 all-gather.5.cloned.1.call-update
  10.2 0.9 convert_reduce_fusion
  11.2 0.7 and_select_fusion.1
  11.9 0.1 select_convert_fusion
  12.0 2.2 convolution_convert_fusion.3
  14.3 7.3 %all-to-all-start = ((bf16[8,32,1280]{2,1,0:T(8,128)(2,1)}), bf16[8,32,1280]{2,1,0:T(8,128)(2,1)S(1)}, u32[]{:S(2)}, u32[]{:S(2)}) async-start(bf16[8,32,1280]{2,1,0:T(8,128)(2,1)} %bitcast.128), calls=%async_computation | async-start | bytes 1310720 | tf_op jit(solution)/shard_map/all_to_all | solution.py:50
  21.6 0.0 copy-done.7
  21.6 0.8 fusion.88
  22.4 0.2 bitcast_compare_fusion
  22.6 20.2 %all-to-all-done = bf16[8,32,1280]{2,1,0:T(8,128)(2,1)S(1)} async-done(((bf16[8,32,1280]{2,1,0:T(8,128)(2,1)}), bf16[8,32,1280]{2,1,0:T(8,128)(2,1)S(1)}, u32[]{:S(2)}, u32[]{:S(2)}) %all-to-all-start) | async-done | bytes 655392 | tf_op jit(solution)/shard_map/all_to_all | solution.py:50
  42.8 0.7 fusion.123
  43.5 0.9 copy.43
  44.5 0.9 copy.42
  45.4 1.2 convolution_convert_fusion.2
  46.6 38.9 %all-gather.3.cloned.1.call-done = bf16[4608,640]{1,0:T(8,128)(2,1)} async-done(((bf16[144,640]{1,0:T(8,128)(2,1)}), bf16[4608,640]{1,0:T(8,128)(2,1)}) %all-gather.3.cloned.1.call-update) | async-done | bytes 5898256 | tf_op jit(solution)/shard_map/all_gather | solution.py:19
  85.4 8.9 %copy.36 = bf16[4,640,1152]{2,1,0:T(8,128)(2,1)} copy(bf16[4,640,1152]{1,2,0:T(8,128)(2,1)} %bitcast.124) | data formatting | bytes 11796480 | tf_op jit(solution)/shard_map/rk,gkn->rgn/dot_general | solution.py:53
  94.3 90.3 %all-gather.5.cloned.1.call-done = bf16[10240,640]{1,0:T(8,128)(2,1)} async-done(((bf16[320,640]{1,0:T(8,128)(2,1)}), bf16[10240,640]{1,0:T(8,128)(2,1)}) %all-gather.5.cloned.1.call-update) | async-done | bytes 13107216 | tf_op jit(solution)/shard_map/all_gather | solution.py:19
  184.7 17.7 %copy.37 = bf16[4,640,2560]{2,1,0:T(8,128)(2,1)} copy(bf16[4,640,2560]{1,2,0:T(8,128)(2,1)} %bitcast.122) | data formatting | bytes 26214400 | tf_op jit(solution)/shard_map/rk,gkn->rgn/dot_general | solution.py:56
  202.4 0.0 copy-done.3
  202.4 0.0 copy-done.12
  202.4 0.0 copy-done.13
  202.4 0.0 copy-start.4
  202.4 15.8 %fusion.12 = (f32[256]{0:T(256)S(1)}, bf16[256,2560]{1,0:T(8,128)(2,1)}) fusion(f32[2560]{0:T(1024)S(1)} %copy-done.12, bf16[2560,2560]{1,0:T(8,128)(2,1)} %bitcast.123, bf16[256,1152]{1,0:T(8,128)(2,1)S(1)} %copy-done.3, bf16[2560,1152]{1,0:T(8,128)(2,1)} %bitcast.125, f32[2560]{0:T(1024)S(1)} %copy-done.13), kind=kOutput, calls=%fused_computation.21 | convolution fusion | flops 4911923200 | bytes 20927488 | tf_op jit(solution)/shard_map/rk,gkn->rgn/dot_general | solution.py:56
  218.2 0.0 copy-done.4
  218.3 3.0 convolution_convert_fusion
  221.2 0.0 copy-done.8
  221.2 0.0 copy-start.10
  221.2 120.1 %all_to_all.22 = bf16[8,1,128,2560]{3,2,1,0:T(8,128)(2,1)S(1)} all-to-all(bf16[8,1,128,2560]{3,2,1,0:T(8,128)(2,1)S(1)} %bitcast.121), channel_id=1, replica_groups=mesh['grp'=4,'ep'=8] {'ep'}, dimensions={0} | all-to-all | bytes 10485760 | tf_op jit(solution)/shard_map/all_to_all | solution.py:79
  341.4 2.4 copy-done.1
  343.7 0.0 copy-done.10
  343.7 4.2 fusion.2
  347.9 10.3 %fusion.4 = bf16[8,1,128,2560]{3,2,1,0:T(8,128)(2,1)} fusion(bf16[1,512,2560]{2,1,0:T(8,128)(2,1)S(1)} %copy-done, bf16[1,2560,512]{2,1,0:T(8,128)(2,1)} %param.22, bf16[8,1,128,2560]{3,2,1,0:T(8,128)(2,1)} %copy-done.1, f32[8,128,512]{2,1,0:T(8,128)} %fusion.2), kind=kOutput, calls=%fused_computation.6 | convolution fusion | flops 5374476288 | bytes 17825792 | tf_op jit(solution)/shard_map/pecf,efd->pecd/dot_general | solution.py:83
  358.3 0.0 copy-start.11
  358.3 4.8 all-to-all-start.2
  363.1 0.1 copy.41
  363.3 0.1 copy.38
  363.4 0.3 iota_compare_fusion
  363.7 0.3 iota_compare_fusion.1
  364.1 1.8 fusion.82
  366.0 112.0 %all-to-all-done.2 = bf16[8,1,128,2560]{3,2,1,0:T(8,128)(2,1)} async-done(((bf16[8,1,128,2560]{3,2,1,0:T(8,128)(2,1)}), bf16[8,1,128,2560]{3,2,1,0:T(8,128)(2,1)}, u32[]{:S(2)}, u32[]{:S(2)}) %all-to-all-start.2) | async-done | bytes 5242912 | tf_op jit(solution)/shard_map/all_to_all | solution.py:86
  478.0 4.1 convolution_multiply_fusion
  482.1 5.2 %fusion.7 = bf16[256,2560]{1,0:T(8,128)(2,1)} fusion(f32[256,2560]{1,0:T(8,128)S(1)} %convolution_multiply_fusion, bf16[1024,2560]{1,0:T(8,128)(2,1)} %bitcast.36, bf16[256,2560]{1,0:T(8,128)(2,1)S(1)} %copy-done.2, f32[256]{0:T(256)S(1)} %bitcast.132, pred[32,8,8,128]{3,2,1,0:T(8,128)(4,1)S(1)} %bitcast.129), kind=kOutput, calls=%fused_computation.16 | convolution fusion | flops 1345454080 | bytes 10748928 | tf_op jit(solution)/shard_map/dot_general | solution.py:92
  (24 shorter events, 0.1 us)
Async XLA Ops:
  6.5 341.4 %copy-start = (bf16[1,512,2560]{2,1,0:T(8,128)(2,1)S(1)}, bf16[1,512,2560]{2,1,0:T(8,128)(2,1)}, u32[]{:S(2)}) copy-start(bf16[1,512,2560]{2,1,0:T(8,128)(2,1)} %param.23) | copy-start | bytes 7864324
  6.5 15.0 %copy-start.7 = (s32[256,2]{0,1:T(2,128)S(1)}, s32[256,2]{0,1:T(2,128)}, u32[]{:S(2)}) copy-start(s32[256,2]{0,1:T(2,128)} %param.14) | copy-start | bytes 6148
  6.5 78.9 %all-gather.3.cloned.1.call-start = ((), (), s32[]{:S(2)}) async-start(), calls=%async_computation.3 | async-start | bytes 6082560 | tf_op jit(solution)/shard_map/all_gather | solution.py:19
  8.4 176.3 %all-gather.5.cloned.1.call-start = ((), (), s32[]{:S(2)}) async-start(), calls=%async_computation.4 | async-start | bytes 13516800 | tf_op jit(solution)/shard_map/all_gather | solution.py:19
  14.3 28.6 %all-to-all-start = ((bf16[8,32,1280]{2,1,0:T(8,128)(2,1)}), bf16[8,32,1280]{2,1,0:T(8,128)(2,1)S(1)}, u32[]{:S(2)}, u32[]{:S(2)}) async-start(bf16[8,32,1280]{2,1,0:T(8,128)(2,1)} %bitcast.128), calls=%async_computation | async-start | bytes 1310720 | tf_op jit(solution)/shard_map/all_to_all | solution.py:50
  184.7 17.7 %copy-start.3 = (bf16[256,1152]{1,0:T(8,128)(2,1)S(1)}, bf16[256,1152]{1,0:T(8,128)(2,1)}, u32[]{:S(2)}) copy-start(bf16[256,1152]{1,0:T(8,128)(2,1)} %convolution_convert_fusion.2) | copy-start | bytes 1769476
  184.7 17.7 %copy-start.12 = (f32[2560]{0:T(1024)S(1)}, f32[2560]{0:T(1024)}, u32[]{:S(2)}) copy-start(f32[2560]{0:T(1024)} %param.18) | copy-start | bytes 30724
  184.7 17.7 %copy-start.13 = (f32[2560]{0:T(1024)S(1)}, f32[2560]{0:T(1024)}, u32[]{:S(2)}) copy-start(f32[2560]{0:T(1024)} %param.16) | copy-start | bytes 30724
  202.4 15.9 %copy-start.4 = (f32[2560]{0:T(1024)S(1)}, f32[2560]{0:T(1024)}, u32[]{:S(2)}) copy-start(f32[2560]{0:T(1024)} %param.19) | copy-start | bytes 30724
  218.2 3.0 copy-start.8
  221.2 122.5 %copy-start.10 = (bf16[1,2560,512]{2,1,0:T(8,128)(2,1)S(1)}, bf16[1,2560,512]{2,1,0:T(8,128)(2,1)}, u32[]{:S(2)}) copy-start(bf16[1,2560,512]{2,1,0:T(8,128)(2,1)} %param.21) | copy-start | bytes 7864324
  341.4 2.4 copy-start.1
  358.3 4.8 copy-start.6
  358.3 5.0 %copy-start.5 = (s32[256,8]{0,1:T(8,128)S(1)}, s32[256,8]{0,1:T(8,128)}, u32[]{:S(2)}) copy-start(s32[256,8]{0,1:T(8,128)} %get-tuple-element.11) | copy-start | bytes 24580
  358.3 5.8 %copy-start.9 = (f32[256]{0:T(256)S(1)}, f32[256]{0:T(256)}, u32[]{:S(2)}) copy-start(f32[256]{0:T(256)} %copy-done.8) | copy-start | bytes 3076
  358.3 5.8 %copy-start.11 = (bf16[2560,8]{0,1:T(8,128)(2,1)S(1)}, bf16[2560,8]{0,1:T(8,128)(2,1)}, u32[]{:S(2)}) copy-start(bf16[2560,8]{0,1:T(8,128)(2,1)} %param.20) | copy-start | bytes 122884
  358.3 119.7 %all-to-all-start.2 = ((bf16[8,1,128,2560]{3,2,1,0:T(8,128)(2,1)}), bf16[8,1,128,2560]{3,2,1,0:T(8,128)(2,1)}, u32[]{:S(2)}, u32[]{:S(2)}) async-start(bf16[8,1,128,2560]{3,2,1,0:T(8,128)(2,1)} %fusion.4), calls=%async_computation.2 | async-start | bytes 10485760 | tf_op jit(solution)/shard_map/all_to_all | solution.py:86
  478.0 4.1 copy-start.2
Sparse Core Ops, SparseCore 0:
  10.2 75.1 all-gather.2
  88.3 96.3 all-gather.4
where the time goes:
time: 496 us; the launch traced here: 494 us
  waiting for transfers between devices  261 us (53%)
  blocking collectives  120 us (24%)
  matrix products  48.7 us (10%)
  local copies, waits for them, and re-layouts  35.4 us (7%)
  between operations  13.6 us (3%)
  starting transfers between devices  12.2 us (2%)
    all_gather x2, waiting for transfers between devices, gather_columns(): full = lax.all_gather(part, ('grp', 'ep'), axis=0, tiled=True)  129 us
    all_to_all x1, blocking collectives, shards(): lax.all_to_all(blocks, 'ep', split_axis=0, concat_axis=0, tiled=True)  120 us
    all_to_all x1, waiting for transfers between devices, shards(): lax.all_to_all(outputs, 'ep', split_axis=0, concat_axis=0, tiled=True)  112 us
    all_to_all x1, waiting for transfers between devices, shards(): lax.all_to_all(sent, 'ep', split_axis=0, concat_axis=0, tiled=True)  20.2 us
    dot_general x1, local copies, waits for them, and re-layouts, shards(): jnp.einsum('rk,gkn->rgn', hidden, second_full, preferred_element_type=F32)  17.7 us
    dot_general x1, matrix products, shards(): jnp.einsum('rk,gkn->rgn', hidden, second_full, preferred_element_type=F32)  15.8 us
    dot_general x1, matrix products, shards(): jnp.einsum('pecf,efd->pecd', activated, w_down, preferred_element_type=F32)  10.3 us
  transfers between devices with their start and end apart: 4, of which 4 were waited for; matrix products, arithmetic and copies ran while one was open for 5% of the time, Pallas kernels for 0%

commit v1 on v0

--- a/solution.py
+++ b/solution.py
@@ -16,7 +16,10 @@
     members = lax.axis_size("grp")
     width = weight.shape[1] // members
     part = lax.dynamic_slice_in_dim(weight, lax.axis_index("grp") * width, width, 1)
-    full = lax.all_gather(part, ("grp", "ep"), axis=0, tiled=True)
+    full = jnp.concatenate(
+        lax.all_to_all(jnp.stack([part] * lax.axis_size(("grp", "ep"))), ("grp", "ep"), 0, 0),
+        axis=0,
+    )
     return full.reshape(members, -1, width)
 
 

time: 496 us -> 777 us (1.57)
  waiting for transfers between devices: 261 us -> 540 us
  between operations: 13.6 us -> 0.23 us
  local copies, waits for them, and re-layouts: 35.4 us -> 45 us
    all_to_all x0 -> x2, waiting for transfers between devices: none -> 412 us  [gather_columns(): lax.all_to_all(jnp.stack([part] * lax.axis_size(('grp', 'ep'))), ('grp',...]
    all_gather x2 -> x0, waiting for transfers between devices: 129 us -> none  [gather_columns(): full = lax.all_gather(part, ('grp', 'ep'), axis=0, tiled=True)]
    another operation x0 -> x2, local copies, waits for them, and re-layouts: none -> 10.5 us  [gather_columns(): jnp.stack([part] * lax.axis_size(('grp', 'ep')))]
  transfers between devices with their start and end apart: 4 -> 4, of which waited for: 4 -> 4; matrix products, arithmetic and copies ran while one was open for 5% -> 2% of each run, Pallas kernels for 0% -> 0%
where the time goes in v1:
time: 777 us; the launch traced here: 776 us
  waiting for transfers between devices  540 us (69%)
  blocking collectives  118 us (15%)
  matrix products  48.7 us (6%)
  local copies, waits for them, and re-layouts  45 us (6%)
  starting transfers between devices  19.8 us (3%)
    all_to_all x2, waiting for transfers between devices, gather_columns(): lax.all_to_all(jnp.stack([part] * lax.axis_size(('grp', 'ep'))), ('grp',...  412 us
    all_to_all x1, blocking collectives, shards(): lax.all_to_all(blocks, 'ep', split_axis=0, concat_axis=0, tiled=True)  118 us
    all_to_all x1, waiting for transfers between devices, shards(): lax.all_to_all(outputs, 'ep', split_axis=0, concat_axis=0, tiled=True)  112 us
    dot_general x1, local copies, waits for them, and re-layouts, shards(): jnp.einsum('rk,gkn->rgn', hidden, second_full, preferred_element_type=F32)  17.7 us
    all_to_all x1, waiting for transfers between devices, shards(): lax.all_to_all(sent, 'ep', split_axis=0, concat_axis=0, tiled=True)  16.4 us
    dot_general x1, matrix products, shards(): jnp.einsum('rk,gkn->rgn', hidden, second_full, preferred_element_type=F32)  15.9 us
  transfers between devices with their start and end apart: 4, of which 4 were waited for; matrix products, arithmetic and copies ran while one was open for 2% of the time, Pallas kernels for 0%

profile of v1, /device:TPU:0, one launch (start us, length us, event | category | flops | bytes accessed | tf_op | source)
XLA Modules:
  0.0 775.5 jit_solution(17703631027830720854)
XLA Ops:
  0.0 0.0 copy-start
  0.0 0.8 and_select_fusion.1
  0.9 0.9 convert_reduce_fusion
  1.8 0.1 select_convert_fusion
  1.9 2.3 convolution_convert_fusion.3
  4.2 7.3 all-to-all-start
  11.5 0.9 constant_dynamic-slice_fusion.1
  12.4 16.4 %all-to-all-done = bf16[8,32,1280]{2,1,0:T(8,128)(2,1)S(1)} async-done(((bf16[8,32,1280]{2,1,0:T(8,128)(2,1)}), bf16[8,32,1280]{2,1,0:T(8,128)(2,1)S(1)}, u32[]{:S(2)}, u32[]{:S(2)}) %all-to-all-start) | async-done | bytes 655392 | tf_op jit(solution)/shard_map/all_to_all | solution.py:53
  28.8 3.0 stack.4
  31.8 3.8 all-to-all-start.1
  35.5 1.8 constant_dynamic-slice_fusion
  37.3 131.9 %all-to-all-done.1 = bf16[32,144,640]{2,1,0:T(8,128)(2,1)} async-done(((bf16[32,144,640]{2,1,0:T(8,128)(2,1)}), bf16[32,144,640]{2,1,0:T(8,128)(2,1)}, u32[]{:S(2)}, u32[]{:S(2)}) %all-to-all-start.1) | async-done | bytes 5898272 | tf_op jit(solution)/shard_map/all_to_all | solution.py:20
  169.3 7.5 stack.5
  176.8 3.9 all-to-all-start.2
  180.7 0.0 copy-done.7
  180.7 0.8 fusion.88
  181.5 0.2 bitcast_compare_fusion
  181.7 0.7 fusion.123
  182.4 0.9 copy.43
  183.4 0.9 copy.42
  184.3 1.2 convolution_convert_fusion.2
  185.5 8.9 %copy.36 = bf16[4,640,1152]{2,1,0:T(8,128)(2,1)} copy(bf16[4,640,1152]{1,2,0:T(8,128)(2,1)} %bitcast.4) | data formatting | bytes 11796480 | tf_op jit(solution)/shard_map/rk,gkn->rgn/dot_general | solution.py:56
  194.4 280.3 %all-to-all-done.2 = bf16[32,320,640]{2,1,0:T(8,128)(2,1)} async-done(((bf16[32,320,640]{2,1,0:T(8,128)(2,1)}), bf16[32,320,640]{2,1,0:T(8,128)(2,1)}, u32[]{:S(2)}, u32[]{:S(2)}) %all-to-all-start.2) | async-done | bytes 13107232 | tf_op jit(solution)/shard_map/all_to_all | solution.py:20
  474.7 17.7 %copy.37 = bf16[4,640,2560]{2,1,0:T(8,128)(2,1)} copy(bf16[4,640,2560]{1,2,0:T(8,128)(2,1)} %bitcast.7) | data formatting | bytes 26214400 | tf_op jit(solution)/shard_map/rk,gkn->rgn/dot_general | solution.py:59
  492.3 0.0 copy-done.3
  492.3 0.0 copy-done.12
  492.3 0.0 copy-done.13
  492.3 0.0 copy-start.4
  492.4 15.9 %fusion.12 = (f32[256]{0:T(256)S(1)}, bf16[256,2560]{1,0:T(8,128)(2,1)}) fusion(f32[2560]{0:T(1024)S(1)} %copy-done.12, bf16[2560,2560]{1,0:T(8,128)(2,1)} %bitcast.122, bf16[256,1152]{1,0:T(8,128)(2,1)S(1)} %copy-done.3, bf16[2560,1152]{1,0:T(8,128)(2,1)} %bitcast.123, f32[2560]{0:T(1024)S(1)} %copy-done.13), kind=kOutput, calls=%fused_computation.21 | convolution fusion | flops 4911923200 | bytes 20927488 | tf_op jit(solution)/shard_map/rk,gkn->rgn/dot_general | solution.py:59
  508.2 0.0 copy-done.4
  508.2 3.0 convolution_convert_fusion
  511.2 0.0 copy-start.10
  511.2 118.5 %all_to_all.32 = bf16[8,1,128,2560]{3,2,1,0:T(8,128)(2,1)S(1)} all-to-all(bf16[8,1,128,2560]{3,2,1,0:T(8,128)(2,1)S(1)} %bitcast.121), channel_id=1, replica_groups=mesh['grp'=4,'ep'=8] {'ep'}, dimensions={0} | all-to-all | bytes 10485760 | tf_op jit(solution)/shard_map/all_to_all | solution.py:82
  629.7 2.3 copy-done.1
  632.0 4.2 fusion.2
  636.2 0.0 copy-done
  636.2 10.3 %fusion.4 = bf16[8,1,128,2560]{3,2,1,0:T(8,128)(2,1)} fusion(bf16[1,512,2560]{2,1,0:T(8,128)(2,1)S(1)} %copy-done, bf16[1,2560,512]{2,1,0:T(8,128)(2,1)} %param.22, bf16[8,1,128,2560]{3,2,1,0:T(8,128)(2,1)} %copy-done.1, f32[8,128,512]{2,1,0:T(8,128)} %fusion.2), kind=kOutput, calls=%fused_computation.6 | convolution fusion | flops 5374476288 | bytes 17825792 | tf_op jit(solution)/shard_map/pecf,efd->pecd/dot_general | solution.py:86
  646.6 0.0 copy-start.11
  646.6 4.8 all-to-all-start.4
  651.4 0.0 copy-done.6
  651.4 0.1 copy.41
  651.6 0.1 copy.38
  651.7 0.3 iota_compare_fusion
  652.1 0.3 iota_compare_fusion.1
  652.4 1.8 fusion.82
  654.3 111.9 %all-to-all-done.4 = bf16[8,1,128,2560]{3,2,1,0:T(8,128)(2,1)} async-done(((bf16[8,1,128,2560]{3,2,1,0:T(8,128)(2,1)}), bf16[8,1,128,2560]{3,2,1,0:T(8,128)(2,1)}, u32[]{:S(2)}, u32[]{:S(2)}) %all-to-all-start.4) | async-done | bytes 5242912 | tf_op jit(solution)/shard_map/all_to_all | solution.py:89
  766.2 4.1 convolution_multiply_fusion
  770.3 5.2 fusion.7
  (24 shorter events, 0.1 us)
Async XLA Ops:
  0.0 636.2 %copy-start = (bf16[1,512,2560]{2,1,0:T(8,128)(2,1)S(1)}, bf16[1,512,2560]{2,1,0:T(8,128)(2,1)}, u32[]{:S(2)}) copy-start(bf16[1,512,2560]{2,1,0:T(8,128)(2,1)} %param.23) | copy-start | bytes 7864324
  4.2 24.6 %all-to-all-start = ((bf16[8,32,1280]{2,1,0:T(8,128)(2,1)}), bf16[8,32,1280]{2,1,0:T(8,128)(2,1)S(1)}, u32[]{:S(2)}, u32[]{:S(2)}) async-start(bf16[8,32,1280]{2,1,0:T(8,128)(2,1)} %bitcast.126), calls=%async_computation | async-start | bytes 1310720 | tf_op jit(solution)/shard_map/all_to_all | solution.py:53
  31.8 137.5 %all-to-all-start.1 = ((bf16[32,144,640]{2,1,0:T(8,128)(2,1)}), bf16[32,144,640]{2,1,0:T(8,128)(2,1)}, u32[]{:S(2)}, u32[]{:S(2)}) async-start(bf16[32,144,640]{2,1,0:T(8,128)(2,1)} %stack.4), calls=%async_computation.1 | async-start | bytes 11796480 | tf_op jit(solution)/shard_map/all_to_all | solution.py:20
  176.8 3.9 copy-start.7
  176.8 297.9 %all-to-all-start.2 = ((bf16[32,320,640]{2,1,0:T(8,128)(2,1)}), bf16[32,320,640]{2,1,0:T(8,128)(2,1)}, u32[]{:S(2)}, u32[]{:S(2)}) async-start(bf16[32,320,640]{2,1,0:T(8,128)(2,1)} %stack.5), calls=%async_computation.2 | async-start | bytes 26214400 | tf_op jit(solution)/shard_map/all_to_all | solution.py:20
  474.7 17.7 %copy-start.3 = (bf16[256,1152]{1,0:T(8,128)(2,1)S(1)}, bf16[256,1152]{1,0:T(8,128)(2,1)}, u32[]{:S(2)}) copy-start(bf16[256,1152]{1,0:T(8,128)(2,1)} %convolution_convert_fusion.2) | copy-start | bytes 1769476
  474.7 17.7 %copy-start.12 = (f32[2560]{0:T(1024)S(1)}, f32[2560]{0:T(1024)}, u32[]{:S(2)}) copy-start(f32[2560]{0:T(1024)} %param.18) | copy-start | bytes 30724
  474.7 17.7 %copy-start.13 = (f32[2560]{0:T(1024)S(1)}, f32[2560]{0:T(1024)}, u32[]{:S(2)}) copy-start(f32[2560]{0:T(1024)} %param.16) | copy-start | bytes 30724
  492.3 15.9 %copy-start.4 = (f32[2560]{0:T(1024)S(1)}, f32[2560]{0:T(1024)}, u32[]{:S(2)}) copy-start(f32[2560]{0:T(1024)} %param.19) | copy-start | bytes 30724
  508.2 3.0 copy-start.8
  511.2 120.8 %copy-start.10 = (bf16[1,2560,512]{2,1,0:T(8,128)(2,1)S(1)}, bf16[1,2560,512]{2,1,0:T(8,128)(2,1)}, u32[]{:S(2)}) copy-start(bf16[1,2560,512]{2,1,0:T(8,128)(2,1)} %param.21) | copy-start | bytes 7864324
  629.7 2.4 copy-start.1
  646.6 4.9 copy-start.6
  646.6 5.0 copy-start.5
  646.6 5.8 copy-start.9
  646.6 5.8 copy-start.11
  646.6 119.6 %all-to-all-start.4 = ((bf16[8,1,128,2560]{3,2,1,0:T(8,128)(2,1)}), bf16[8,1,128,2560]{3,2,1,0:T(8,128)(2,1)}, u32[]{:S(2)}, u32[]{:S(2)}) async-start(bf16[8,1,128,2560]{3,2,1,0:T(8,128)(2,1)} %fusion.4), calls=%async_computation.4 | async-start | bytes 10485760 | tf_op jit(solution)/shard_map/all_to_all | solution.py:89
  766.2 4.1 copy-start.2
